TPU v7x, 32 devices: a whole 2x2x4 slice. The times are simulated.
32 devices in a mesh: area: 8 (over z, x), scen: 4 (over y, core).
Axes of the slice: x: 2, y: 2, z: 4, core: 2. Of those that a mesh axis runs over, the one named last changes fastest.
Arguments:
- injection: float32 [8, 128, 4096], P('area', 'scen'), may hold values from -6 to 6
- kkt_factor: bfloat16 [8, 4096, 4096], P('area', 'scen'), may hold values from -0.09375 to 0.09375
- dual_price: float32 [8, 128, 512], P('area', 'scen'), may hold values from -6 to 6
- area_size: int32 [8], replicated, may hold values from 1024 to 4096, as said below
- bnd_bus: int32 [8, 512], replicated, may hold values from 0 to 4095, as said below
- peer_end: int32 [8, 512], replicated, may hold values from 0 to 4095, as said below
Outputs:
- angles: float32 [8, 128, 4096], P('area', 'scen')
- dual_out: float32 [8, 128, 512], P('area', 'scen')
- consensus: float32 [8, 128, 512], P('area', 'scen')
Inputs may be any that keep to these rules, and one draw needn't show every extreme that they name: `area_size`: one area has exactly 4096 live buses and another exactly 1024. `bnd_bus`: the buses of one area's ends are distinct and lie below that area's size; they include bus 0 and the area's last live bus. peer_end is a pairing: the peer of an end's peer is the end itself, and the two ends lie in different areas. The ends of area a form 4 tie sets of 128 consecutive ends; tie set g of area a is paired whole with tie set g of area a XOR s_g, where s_g is nonzero, the same for all areas, and the 4 values s_g differ.
All inputs are finite; a program needn't handle non-finite values.
Results may differ from a plain program's by a relative error of at most 0.0043.
Values may be sent and summed in bfloat16 or wider, within the bound.
No kernel may reach another device: no remote copies, remote signals or barrier semaphores. Data moves between devices by JAX's collectives and lax.ppermute only.
A program may use at most 128 MiB of HBM per device.

v0:
```python
import jax
import jax.numpy as jnp
from jax import lax
from jax.sharding import PartitionSpec as P

CAP = 128
ITERS = 2
PENALTY = 1.5
PROXIMAL = 0.5


def shards(injection, kkt_factor, dual_price, area_size, bnd_bus, peer_end):
    area_id = lax.axis_index("area")
    band_index = lax.axis_index("scen")
    areas_all = lax.axis_size("area")
    factor = kkt_factor[0]
    band_rows = factor.shape[0]
    width = factor.shape[1]
    columns = injection.shape[1]
    ends_total = bnd_bus.shape[1]
    slot_count = CAP
    groups = ends_total // slot_count
    size_here = area_size[area_id]
    live_mask = (jnp.arange(width) < size_here).astype(jnp.float32)
    band_mask = (band_index * band_rows + jnp.arange(band_rows) < size_here).astype(jnp.float32)[
        None, :
    ]
    buses = bnd_bus[area_id]
    peers = peer_end[area_id]
    group_mate = peers.reshape(groups, slot_count)[:, 0] // ends_total
    group_ids = jnp.arange(groups)
    owner_dev = 8 * (jnp.minimum(area_id, group_mate) // 8) + group_ids
    injection_here = injection[0]
    dual_here = dual_price[0]
    consensus = jnp.zeros((columns, ends_total), jnp.float32)
    held = jnp.zeros((columns, areas_all, slot_count), jnp.float32)
    angles = jnp.zeros((columns, width), jnp.float32)
    for sweep in range(ITERS):
        pushed = dual_here - PENALTY * consensus
        spread = jnp.zeros((columns, width), jnp.float32).at[:, buses].add(pushed)
        right_side = ((injection_here - spread) * live_mask).astype(jnp.bfloat16)
        projected = jnp.dot(
            lax.all_gather(right_side, "scen", axis=0, tiled=True),
            factor.T,
            preferred_element_type=jnp.float32,
        )
        projected = (projected * band_mask).astype(jnp.bfloat16)
        angles = (
            lax.psum_scatter(
                jnp.dot(projected, factor, preferred_element_type=jnp.float32),
                "scen",
                scatter_dimension=0,
                tiled=True,
            )
            * live_mask
        )
        end_angles = angles[:, buses]
        stacked = jnp.stack([end_angles, dual_here]).reshape(2, columns, groups, slot_count)
        source_group = jnp.minimum(area_id % 8, groups - 1)
        source_peers = lax.dynamic_slice_in_dim(peer_end, source_group * slot_count, slot_count, 1)
        source_flat = (source_peers // ends_total * slot_count + source_peers % slot_count).reshape(
            -1
        )
        outgoing = (
            jnp.zeros((2, columns, areas_all, slot_count), jnp.float32)
            .at[:, :, owner_dev]
            .set(stacked)
        )
        incoming = lax.all_to_all(outgoing, "area", split_axis=2, concat_axis=2, tiled=True)
        flat_in = incoming.reshape(2, columns, areas_all * slot_count)
        mate_vals = flat_in[:, :, source_flat].reshape(2, columns, areas_all, slot_count)
        held = (
            PENALTY * (incoming[0] + mate_vals[0]) + (incoming[1] + mate_vals[1]) + PROXIMAL * held
        ) / (2.0 * PENALTY + PROXIMAL)
        returned = lax.all_to_all(held, "area", split_axis=1, concat_axis=1, tiled=True)
        consensus = returned[:, owner_dev, :].reshape(columns, ends_total)
        dual_here = dual_here + PENALTY * (end_angles - consensus)
    return (angles[None], dual_here[None], consensus[None])


def solution(mesh):
    return jax.shard_map(
        shards,
        mesh=mesh,
        in_specs=(
            P("area", "scen", None),
            P("area", "scen", None),
            P("area", "scen", None),
            P(),
            P(),
            P(),
        ),
        out_specs=(P("area", "scen", None), P("area", "scen", None), P("area", "scen", None)),
        check_vma=False,
    )
```

profile of v0, /device:TPU:0, one launch (start us, length us, event | category | flops | bytes accessed | tf_op | source)
XLA Modules:
  0.0 220.0 jit_solution(10403555091593370773)
XLA Ops:
  7.2 1.2 dynamic_slice.14
  8.5 0.7 compare_select_fusion.1
  9.2 0.7 fusion.53
  9.8 1.0 copy.107
  10.8 2.8 %scatter_custom_fusion = f32[32,4096]{0,1:T(8,128)S(1)} fusion(s32[512]{0:T(512)S(1)} %bitcast.168, f32[]{:T(128)} %constant.82.clone.1, f32[1,32,512]{1,2,0:T(8,128)S(1)} %copy.107), kind=kCustom, calls=%fused_computation.24 | custom fusion | flops 16384 | bytes 786436 | tf_op jit(solution)/shard_map/scatter-add | solution.py:40
  13.6 0.6 copy.108
  14.2 0.8 fusion.29
  15.0 0.7 fusion.57
  15.7 18.9 %all-gather.3.cloned.1.call-done = bf16[128,4096]{1,0:T(8,128)(2,1)} async-done(((bf16[32,4096]{1,0:T(8,128)(2,1)}), bf16[128,4096]{1,0:T(8,128)(2,1)}) %all-gather.3.cloned.1.call-update) | async-done | bytes 1048592 | tf_op jit(solution)/shard_map/all_gather | solution.py:43
  34.6 11.4 %fusion.4 = f32[128,4096]{1,0:T(8,128)} fusion(bf16[1,1024,4096]{2,1,0:T(8,128)(2,1)} %param.7, bf16[128,4096]{1,0:T(8,128)(2,1)} %all-gather.3.cloned.1.call-done, f32[1024]{0:T(1024)S(1)} %fusion.57), kind=kOutput, calls=%fused_computation.14 | convolution fusion | flops 2147745792 | bytes 11538432 | tf_op jit(solution)/shard_map/dot_general | solution.py:50
  46.0 0.7 constant_dynamic-slice_fusion
  46.9 30.4 %reduce-scatter.3.cloned.1.call-done = f32[32,4096]{1,0:T(8,128)} async-done(((f32[128,4096]{1,0:T(8,128)}), f32[32,4096]{1,0:T(8,128)}) %reduce-scatter.3.cloned.1.call-update) | async-done | bytes 524304 | tf_op jit(solution)/shard_map/reduce_scatter | solution.py:49
  77.3 1.1 broadcast_multiply_fusion.1
  78.4 0.6 copy.109
  79.0 1.0 gather_fusion
  80.2 0.7 scatter_fusion
  80.9 0.7 copy.112
  81.6 5.5 %all-to-all-start = ((f32[2,32,8,128]{3,1,0,2:T(8,128)}), f32[2,32,8,128]{3,1,0,2:T(8,128)S(1)}, u32[]{:S(2)}, u32[]{:S(2)}) async-start(f32[2,32,8,128]{3,1,0,2:T(8,128)} %copy.112), calls=%async_computation.1 | async-start | bytes 524288 | tf_op jit(solution)/shard_map/all_to_all | solution.py:69
  87.2 0.7 fusion.56
  87.9 8.0 %all-to-all-done = f32[2,32,8,128]{3,1,0,2:T(8,128)S(1)} async-done(((f32[2,32,8,128]{3,1,0,2:T(8,128)}), f32[2,32,8,128]{3,1,0,2:T(8,128)S(1)}, u32[]{:S(2)}, u32[]{:S(2)}) %all-to-all-start) | async-done | bytes 262176 | tf_op jit(solution)/shard_map/all_to_all | solution.py:69
  95.9 0.6 copy.140
  96.5 3.6 %gather_fusion.1 = f32[1024,2,32]{2,1,0:T(2,128)S(1)} fusion(f32[2,32,1024]{1,0,2:T(2,128)S(1)} %bitcast.162, s32[1024]{0:T(1024)S(1)} %broadcast_clamp_fusion), kind=kCustom, calls=%fused_computation.1 | custom fusion | bytes 528384 | tf_op jit(solution)/shard_map/gather | solution.py:71
  100.0 0.8 fusion.70
  101.2 0.7 broadcast_multiply_fusion.2
  101.9 3.6 %all-to-all-start.1 = ((f32[32,8,128]{2,0,1:T(8,128)}), f32[32,8,128]{2,0,1:T(8,128)S(1)}, u32[]{:S(2)}, u32[]{:S(2)}) async-start(f32[32,8,128]{2,0,1:T(8,128)} %get-tuple-element.18), calls=%async_computation.2 | async-start | bytes 262144 | tf_op jit(solution)/shard_map/all_to_all | solution.py:75
  105.6 7.3 %all-to-all-done.1 = f32[32,8,128]{2,0,1:T(8,128)S(1)} async-done(((f32[32,8,128]{2,0,1:T(8,128)}), f32[32,8,128]{2,0,1:T(8,128)S(1)}, u32[]{:S(2)}, u32[]{:S(2)}) %all-to-all-start.1) | async-done | bytes 131104 | tf_op jit(solution)/shard_map/all_to_all | solution.py:75
  112.9 0.6 gather_fusion.2
  113.6 2.9 %scatter_custom_fusion.2 = f32[32,4096]{0,1:T(8,128)S(1)} fusion(s32[512]{0:T(512)} %bitcast.170, f32[]{:T(128)} %constant.82.clone.1, f32[32,512]{0,1:T(8,128)S(1)} %fusion.40), kind=kCustom, calls=%fused_computation.22 | custom fusion | flops 16384 | bytes 590336 | tf_op jit(solution)/shard_map/scatter-add | solution.py:40
  116.5 1.4 copy.122
  117.9 2.0 fusion.31
  120.1 13.5 %all-gather.5.cloned.1.call-done = bf16[128,4096]{1,0:T(8,128)(2,1)} async-done(((bf16[32,4096]{1,0:T(8,128)(2,1)}), bf16[128,4096]{1,0:T(8,128)(2,1)}) %all-gather.5.cloned.1.call-update) | async-done | bytes 1048592 | tf_op jit(solution)/shard_map/all_gather | solution.py:43
  133.6 11.4 %fusion = f32[128,4096]{1,0:T(8,128)} fusion(bf16[1,1024,4096]{2,1,0:T(8,128)(2,1)} %param.7, bf16[128,4096]{1,0:T(8,128)(2,1)} %all-gather.5.cloned.1.call-done, f32[1024]{0:T(1024)S(1)} %fusion.57), kind=kOutput, calls=%fused_computation.10 | convolution fusion | flops 2147745792 | bytes 11538432 | tf_op jit(solution)/shard_map/dot_general | solution.py:50
  145.2 31.2 %reduce-scatter.5.cloned.1.call-done = f32[32,4096]{1,0:T(8,128)} async-done(((f32[128,4096]{1,0:T(8,128)}), f32[32,4096]{1,0:T(8,128)}) %reduce-scatter.5.cloned.1.call-update) | async-done | bytes 524304 | tf_op jit(solution)/shard_map/reduce_scatter | solution.py:49
  176.4 1.1 broadcast_multiply_fusion
  177.5 0.6 copy.125
  178.1 1.0 gather_fusion.3
  179.3 0.8 scatter_fusion.1
  180.1 14.0 %all_to_all.20 = f32[2,32,8,128]{3,1,0,2:T(8,128)S(1)} all-to-all(f32[2,32,8,128]{3,1,0,2:T(8,128)S(1)} %copy.128), channel_id=1, replica_groups=mesh['area'=8,'scen'=4] {'area'}, dimensions={2} | all-to-all | bytes 524288 | tf_op jit(solution)/shard_map/all_to_all | solution.py:69
  194.2 0.6 copy.145
  194.8 3.6 %gather_fusion.4 = f32[1024,2,32]{2,1,0:T(2,128)S(1)} fusion(f32[2,32,1024]{1,0,2:T(2,128)S(1)} %bitcast.161, s32[1024]{0:T(1024)S(1)} %copy-done.4), kind=kCustom, calls=%fused_computation.4 | custom fusion | bytes 528384 | tf_op jit(solution)/shard_map/gather | solution.py:71
  198.3 0.8 fusion.69
  199.5 0.7 fusion.46
  200.2 3.6 %all-to-all-start.3 = ((f32[32,8,128]{2,0,1:T(8,128)}), f32[32,8,128]{2,0,1:T(8,128)S(1)}, u32[]{:S(2)}, u32[]{:S(2)}) async-start(f32[32,8,128]{2,0,1:T(8,128)} %fusion.46), calls=%async_computation.5 | async-start | bytes 262144 | tf_op jit(solution)/shard_map/all_to_all | solution.py:75
  203.8 0.8 fusion.73
  204.6 6.5 %all-to-all-done.3 = f32[32,8,128]{2,0,1:T(8,128)S(1)} async-done(((f32[32,8,128]{2,0,1:T(8,128)}), f32[32,8,128]{2,0,1:T(8,128)S(1)}, u32[]{:S(2)}, u32[]{:S(2)}) %all-to-all-start.3) | async-done | bytes 131104 | tf_op jit(solution)/shard_map/all_to_all | solution.py:75
  211.1 0.7 gather_fusion.5
  212.0 0.7 copy.138
  212.7 0.7 copy.139
  (51 shorter events, 2.1 us)
Async XLA Ops:
  7.2 27.4 %all-gather.3.cloned.1.call-start = ((), (), s32[]{:S(2)}) async-start(), calls=%async_computation.6 | async-start | bytes 1310720 | tf_op jit(solution)/shard_map/all_gather | solution.py:43
  9.2 37.6 %copy-start.8 = (s32[512,1]{0,1:T(1,128)}, s32[512,1]{0,1:T(1,128)S(1)}, u32[]{:S(2)}) copy-start(s32[512,1]{0,1:T(1,128)S(1)} %compare_select_fusion.1) | copy-start | bytes 6148
  10.8 3.4 %copy-start.1 = (f32[1,32,4096]{2,1,0:T(8,128)S(1)}, f32[1,32,4096]{2,1,0:T(8,128)}, u32[]{:S(2)}) copy-start(f32[1,32,4096]{2,1,0:T(8,128)} %param.6) | copy-start | bytes 1572868
  15.0 62.4 %reduce-scatter.3.cloned.1.call-start = ((), (), s32[]{:S(2)}) async-start(), calls=%async_computation.7 | async-start | bytes 2621440 | tf_op jit(solution)/shard_map/reduce_scatter | solution.py:49
  46.0 0.9 copy-start.2
  46.8 33.3 %copy-start.5 = (s32[1024]{0:T(1024)}, s32[1024]{0:T(1024)S(1)}, u32[]{:S(2)}) copy-start(s32[1024]{0:T(1024)S(1)} %pad_clamp_fusion.1) | copy-start | bytes 12292
  46.9 58.7 %copy-start.7 = (s32[4]{0:T(128)}, s32[4]{0:T(128)S(1)}, u32[]{:S(2)}) copy-start(s32[4]{0:T(128)S(1)} %fusion.65) | copy-start | bytes 52
  81.6 14.3 %all-to-all-start = ((f32[2,32,8,128]{3,1,0,2:T(8,128)}), f32[2,32,8,128]{3,1,0,2:T(8,128)S(1)}, u32[]{:S(2)}, u32[]{:S(2)}) async-start(f32[2,32,8,128]{3,1,0,2:T(8,128)} %copy.112), calls=%async_computation.1 | async-start | bytes 524288 | tf_op jit(solution)/shard_map/all_to_all | solution.py:69
  87.9 13.2 %copy-start.3 = (s32[1024]{0:T(1024)}, s32[1024]{0:T(1024)S(1)}, u32[]{:S(2)}) copy-start(s32[1024]{0:T(1024)S(1)} %broadcast_clamp_fusion) | copy-start | bytes 12292
  101.9 10.9 %all-to-all-start.1 = ((f32[32,8,128]{2,0,1:T(8,128)}), f32[32,8,128]{2,0,1:T(8,128)S(1)}, u32[]{:S(2)}, u32[]{:S(2)}) async-start(f32[32,8,128]{2,0,1:T(8,128)} %get-tuple-element.18), calls=%async_computation.2 | async-start | bytes 262144 | tf_op jit(solution)/shard_map/all_to_all | solution.py:75
  105.5 28.1 %all-gather.5.cloned.1.call-start = ((), (), s32[]{:S(2)}) async-start(), calls=%async_computation.8 | async-start | bytes 1310720 | tf_op jit(solution)/shard_map/all_gather | solution.py:43
  105.6 12.3 %copy-start.9 = (s32[1024]{0:T(1024)}, s32[1024]{0:T(1024)S(1)}, u32[]{:S(2)}) copy-start(s32[1024]{0:T(1024)S(1)} %pad_clamp_fusion) | copy-start | bytes 12292
  119.9 56.5 %reduce-scatter.5.cloned.1.call-start = ((), (), s32[]{:S(2)}) async-start(), calls=%async_computation.9 | async-start | bytes 2621440 | tf_op jit(solution)/shard_map/reduce_scatter | solution.py:49
  145.1 33.0 %copy-start.6 = (s32[1024]{0:T(1024)S(1)}, s32[1024]{0:T(1024)}, u32[]{:S(2)}) copy-start(s32[1024]{0:T(1024)} %copy-done.5) | copy-start | bytes 12292
  179.1 15.6 %copy-start.4 = (s32[1024]{0:T(1024)S(1)}, s32[1024]{0:T(1024)}, u32[]{:S(2)}) copy-start(s32[1024]{0:T(1024)} %copy-done.3) | copy-start | bytes 12292
  198.3 5.5 %copy-start = (f32[32,4096]{1,0:T(8,128)S(1)}, f32[32,4096]{1,0:T(8,128)}, u32[]{:S(2)}) copy-start(f32[32,4096]{1,0:T(8,128)} %reduce-scatter.5.cloned.1.call-done) | copy-start | bytes 1572868
  200.2 10.9 %all-to-all-start.3 = ((f32[32,8,128]{2,0,1:T(8,128)}), f32[32,8,128]{2,0,1:T(8,128)S(1)}, u32[]{:S(2)}, u32[]{:S(2)}) async-start(f32[32,8,128]{2,0,1:T(8,128)} %fusion.46), calls=%async_computation.5 | async-start | bytes 262144 | tf_op jit(solution)/shard_map/all_to_all | solution.py:75
Sparse Core Ops, SparseCore 0:
  15.1 19.4 all-gather.2
  46.1 31.1 reduce-scatter.2
  120.0 13.5 all-gather.4
  145.2 31.1 reduce-scatter.4
where the time goes:
time: 221 us; the launch traced here: 220 us
  waiting for transfers between devices  116 us (52%)
  local copies, waits for them, and re-layouts  24.3 us (11%)
  matrix products  22.8 us (10%)
  other arithmetic  15.9 us (7%)
  between operations  14.2 us (6%)
  blocking collectives  14 us (6%)
  starting transfers between devices  13 us (6%)
    reduce_scatter x2, waiting for transfers between devices, shards(): lax.psum_scatter(jnp.dot(projected, factor, preferred_element_type=jnp.fl...  61.6 us
    all_gather x2, waiting for transfers between devices, shards(): lax.all_gather(right_side, 'scen', axis=0, tiled=True)  32.3 us
    dot_general x2, matrix products, shards(): jnp.dot(projected, factor, preferred_element_type=jnp.float32)  22.8 us
    all_to_all x1, blocking collectives, shards(): lax.all_to_all(outgoing, 'area', split_axis=2, concat_axis=2, tiled=True)  14 us
    all_to_all x2, waiting for transfers between devices, shards(): lax.all_to_all(held, 'area', split_axis=1, concat_axis=1, tiled=True)  13.8 us
    all_to_all x1, waiting for transfers between devices, shards(): lax.all_to_all(outgoing, 'area', split_axis=2, concat_axis=2, tiled=True)  8.02 us
    all_to_all x2, starting transfers between devices, shards(): lax.all_to_all(held, 'area', split_axis=1, concat_axis=1, tiled=True)  7.17 us
    gather x2, local copies, waits for them, and re-layouts, shards(): flat_in[:, :, source_flat].reshape(2, columns, areas_all, slot_count)  7.11 us
  transfers between devices with their start and end apart: 7, of which 7 were waited for; matrix products, arithmetic and copies ran while one was open for 1% of the time, Pallas kernels for 0%

commit v1 on v0

--- a/solution.py
+++ b/solution.py
@@ -72,7 +72,10 @@
         held = (
             PENALTY * (incoming[0] + mate_vals[0]) + (incoming[1] + mate_vals[1]) + PROXIMAL * held
         ) / (2.0 * PENALTY + PROXIMAL)
-        returned = lax.all_to_all(held, "area", split_axis=1, concat_axis=1, tiled=True)
+        devices = lax.axis_size("area")
+        blocks = jnp.stack(jnp.split(held, devices, axis=1), axis=0)
+        blocks = lax.all_to_all(blocks, "area", split_axis=0, concat_axis=0)
+        returned = jnp.concatenate(blocks, axis=1)
         consensus = returned[:, owner_dev, :].reshape(columns, ends_total)
         dual_here = dual_here + PENALTY * (end_angles - consensus)
     return (angles[None], dual_here[None], consensus[None])

time: 221 us -> 230 us (1.041)
  local copies, waits for them, and re-layouts: 24.3 us -> 34.6 us
    unnamed x23 -> x37, local copies, waits for them, and re-layouts: 2.49 us -> 10.9 us
where the time goes in v1:
time: 230 us; the launch traced here: 229 us
  waiting for transfers between devices  116 us (50%)
  local copies, waits for them, and re-layouts  34.6 us (15%)
  matrix products  22.8 us (10%)
  other arithmetic  15 us (7%)
  between operations  14.3 us (6%)
  blocking collectives  14.1 us (6%)
  starting transfers between devices  12.8 us (6%)
    reduce_scatter x2, waiting for transfers between devices, shards(): lax.psum_scatter(jnp.dot(projected, factor, preferred_element_type=jnp.fl...  61.6 us
    all_gather x2, waiting for transfers between devices, shards(): lax.all_gather(right_side, 'scen', axis=0, tiled=True)  32.5 us
    dot_general x2, matrix products, shards(): jnp.dot(projected, factor, preferred_element_type=jnp.float32)  22.8 us
    all_to_all x1, blocking collectives, shards(): lax.all_to_all(outgoing, 'area', split_axis=2, concat_axis=2, tiled=True)  14.1 us
    all_to_all x2, waiting for transfers between devices, shards(): blocks = lax.all_to_all(blocks, 'area', split_axis=0, concat_axis=0)  13.8 us
    unnamed x37, local copies, waits for them, and re-layouts  10.9 us
    all_to_all x1, waiting for transfers between devices, shards(): lax.all_to_all(outgoing, 'area', split_axis=2, concat_axis=2, tiled=True)  8.02 us
    gather x2, local copies, waits for them, and re-layouts, shards(): flat_in[:, :, source_flat].reshape(2, columns, areas_all, slot_count)  7.6 us
  transfers between devices with their start and end apart: 7, of which 7 were waited for; matrix products, arithmetic and copies ran while one was open for 1% of the time, Pallas kernels for 0%

profile of v1, /device:TPU:0, one launch (start us, length us, event | category | flops | bytes accessed | tf_op | source)
XLA Modules:
  0.0 229.5 jit_solution(4439129182628111527)
XLA Ops:
  7.2 1.2 dynamic_slice.14
  8.5 0.7 compare_select_fusion.1
  9.2 0.7 fusion.53
  9.8 1.0 copy.78
  10.8 2.8 %scatter_custom_fusion = f32[32,4096]{0,1:T(8,128)S(1)} fusion(s32[512]{0:T(512)S(1)} %bitcast.228, f32[]{:T(128)} %constant.82.clone.1, f32[1,32,512]{1,2,0:T(8,128)S(1)} %copy.78), kind=kCustom, calls=%fused_computation.24 | custom fusion | flops 16384 | bytes 786436 | tf_op jit(solution)/shard_map/scatter-add | solution.py:40
  14.2 0.8 fusion.29
  15.0 0.7 fusion.57
  15.7 18.9 %all-gather.3.cloned.1.call-done = bf16[128,4096]{1,0:T(8,128)(2,1)} async-done(((bf16[32,4096]{1,0:T(8,128)(2,1)}), bf16[128,4096]{1,0:T(8,128)(2,1)}) %all-gather.3.cloned.1.call-update) | async-done | bytes 1048592 | tf_op jit(solution)/shard_map/all_gather | solution.py:43
  34.6 11.4 %fusion.4 = f32[128,4096]{1,0:T(8,128)} fusion(bf16[1,1024,4096]{2,1,0:T(8,128)(2,1)} %param.7, bf16[128,4096]{1,0:T(8,128)(2,1)} %all-gather.3.cloned.1.call-done, f32[1024]{0:T(1024)S(1)} %fusion.57), kind=kOutput, calls=%fused_computation.14 | convolution fusion | flops 2147745792 | bytes 11538432 | tf_op jit(solution)/shard_map/dot_general | solution.py:50
  46.0 0.7 constant_dynamic-slice_fusion
  46.9 30.4 %reduce-scatter.3.cloned.1.call-done = f32[32,4096]{1,0:T(8,128)} async-done(((f32[128,4096]{1,0:T(8,128)}), f32[32,4096]{1,0:T(8,128)}) %reduce-scatter.3.cloned.1.call-update) | async-done | bytes 524304 | tf_op jit(solution)/shard_map/reduce_scatter | solution.py:49
  77.3 1.1 broadcast_multiply_fusion.1
  79.0 1.0 gather_fusion
  80.2 0.7 scatter_fusion
  80.9 0.7 copy.83
  81.6 5.5 %all-to-all-start = ((f32[2,32,8,128]{3,1,0,2:T(8,128)}), f32[2,32,8,128]{3,1,0,2:T(8,128)S(1)}, u32[]{:S(2)}, u32[]{:S(2)}) async-start(f32[2,32,8,128]{3,1,0,2:T(8,128)} %copy.83), calls=%async_computation.1 | async-start | bytes 524288 | tf_op jit(solution)/shard_map/all_to_all | solution.py:69
  87.2 0.7 fusion.56
  87.9 8.0 %all-to-all-done = f32[2,32,8,128]{3,1,0,2:T(8,128)S(1)} async-done(((f32[2,32,8,128]{3,1,0,2:T(8,128)}), f32[2,32,8,128]{3,1,0,2:T(8,128)S(1)}, u32[]{:S(2)}, u32[]{:S(2)}) %all-to-all-start) | async-done | bytes 262176 | tf_op jit(solution)/shard_map/all_to_all | solution.py:69
  96.5 3.6 %gather_fusion.1 = f32[1024,2,32]{2,1,0:T(2,128)S(1)} fusion(f32[2,32,1024]{1,0,2:T(2,128)S(1)} %bitcast.204, s32[1024]{0:T(1024)S(1)} %broadcast_clamp_fusion), kind=kCustom, calls=%fused_computation.1 | custom fusion | bytes 528384 | tf_op jit(solution)/shard_map/gather | solution.py:71
  100.0 0.8 fusion.70
  101.6 0.6 constant_dynamic-update-slice_fusion.7
  102.2 0.6 constant_dynamic-update-slice_fusion.6
  102.8 0.6 constant_dynamic-update-slice_fusion.5
  103.4 0.6 constant_dynamic-update-slice_fusion.4
  104.0 0.6 constant_dynamic-update-slice_fusion.3
  104.6 0.6 constant_dynamic-update-slice_fusion.2
  105.2 0.6 constant_dynamic-update-slice_fusion.1
  106.4 3.6 %all-to-all-start.1 = ((f32[8,32,1,128]{3,1,2,0:T(8,128)}), f32[8,32,1,128]{3,1,2,0:T(8,128)S(1)}, u32[]{:S(2)}, u32[]{:S(2)}) async-start(f32[8,32,1,128]{3,1,2,0:T(8,128)} %constant_dynamic-update-slice_fusion), calls=%async_computation.2 | async-start | bytes 262144 | tf_op jit(solution)/shard_map/all_to_all | solution.py:77
  110.1 7.3 %all-to-all-done.1 = f32[8,32,1,128]{3,1,2,0:T(8,128)S(1)} async-done(((f32[8,32,1,128]{3,1,2,0:T(8,128)}), f32[8,32,1,128]{3,1,2,0:T(8,128)S(1)}, u32[]{:S(2)}, u32[]{:S(2)}) %all-to-all-start.1) | async-done | bytes 131104 | tf_op jit(solution)/shard_map/all_to_all | solution.py:77
  118.1 3.1 %scatter_custom_fusion.2 = f32[32,4096]{0,1:T(8,128)S(1)} fusion(s32[512]{0:T(512)} %bitcast.230, f32[]{:T(128)} %constant.82.clone.1, f32[32,512]{0,1:T(8,128)S(1)} %fusion.40), kind=kCustom, calls=%fused_computation.22 | custom fusion | flops 16384 | bytes 590336 | tf_op jit(solution)/shard_map/scatter-add | solution.py:40
  121.2 1.4 copy.98
  122.6 2.0 fusion.31
  124.6 13.7 %all-gather.5.cloned.1.call-done = bf16[128,4096]{1,0:T(8,128)(2,1)} async-done(((bf16[32,4096]{1,0:T(8,128)(2,1)}), bf16[128,4096]{1,0:T(8,128)(2,1)}) %all-gather.5.cloned.1.call-update) | async-done | bytes 1048592 | tf_op jit(solution)/shard_map/all_gather | solution.py:43
  138.3 11.4 %fusion = f32[128,4096]{1,0:T(8,128)} fusion(bf16[1,1024,4096]{2,1,0:T(8,128)(2,1)} %param.7, bf16[128,4096]{1,0:T(8,128)(2,1)} %all-gather.5.cloned.1.call-done, f32[1024]{0:T(1024)S(1)} %fusion.57), kind=kOutput, calls=%fused_computation.10 | convolution fusion | flops 2147745792 | bytes 11538432 | tf_op jit(solution)/shard_map/dot_general | solution.py:50
  149.9 31.1 %reduce-scatter.5.cloned.1.call-done = f32[32,4096]{1,0:T(8,128)} async-done(((f32[128,4096]{1,0:T(8,128)}), f32[32,4096]{1,0:T(8,128)}) %reduce-scatter.5.cloned.1.call-update) | async-done | bytes 524304 | tf_op jit(solution)/shard_map/reduce_scatter | solution.py:49
  181.0 1.1 broadcast_multiply_fusion
  182.7 1.0 gather_fusion.3
  183.9 0.7 scatter_fusion.1
  184.6 14.1 %all_to_all.20 = f32[2,32,8,128]{3,1,0,2:T(8,128)S(1)} all-to-all(f32[2,32,8,128]{3,1,0,2:T(8,128)S(1)} %copy.104), channel_id=1, replica_groups=mesh['area'=8,'scen'=4] {'area'}, dimensions={2} | all-to-all | bytes 524288 | tf_op jit(solution)/shard_map/all_to_all | solution.py:69
  199.3 4.0 %gather_fusion.4 = f32[1024,2,32]{2,1,0:T(2,128)S(1)} fusion(f32[2,32,1024]{1,0,2:T(2,128)S(1)} %bitcast.203, s32[1024]{0:T(1024)} %copy-done.3), kind=kCustom, calls=%fused_computation.4 | custom fusion | bytes 528384 | tf_op jit(solution)/shard_map/gather | solution.py:71
  203.3 0.8 fusion.69
  207.9 0.6 constant_dynamic-update-slice_fusion.10
  209.7 3.6 %all-to-all-start.3 = ((f32[8,32,1,128]{3,1,2,0:T(8,128)}), f32[8,32,1,128]{3,1,2,0:T(8,128)S(1)}, u32[]{:S(2)}, u32[]{:S(2)}) async-start(f32[8,32,1,128]{3,1,2,0:T(8,128)} %constant_dynamic-update-slice_fusion.8), calls=%async_computation.5 | async-start | bytes 262144 | tf_op jit(solution)/shard_map/all_to_all | solution.py:77
  213.3 0.8 fusion.77
  214.1 6.5 %all-to-all-done.3 = f32[8,32,1,128]{3,1,2,0:T(8,128)S(1)} async-done(((f32[8,32,1,128]{3,1,2,0:T(8,128)}), f32[8,32,1,128]{3,1,2,0:T(8,128)S(1)}, u32[]{:S(2)}, u32[]{:S(2)}) %all-to-all-start.3) | async-done | bytes 131104 | tf_op jit(solution)/shard_map/all_to_all | solution.py:77
  220.6 0.7 gather_fusion.5
  221.5 0.7 copy.119
  222.2 0.7 copy.120
  (71 shorter events, 10.8 us)
Async XLA Ops:
  7.2 27.4 %all-gather.3.cloned.1.call-start = ((), (), s32[]{:S(2)}) async-start(), calls=%async_computation.6 | async-start | bytes 1310720 | tf_op jit(solution)/shard_map/all_gather | solution.py:43
  9.2 37.6 %copy-start.8 = (s32[512,1]{0,1:T(1,128)}, s32[512,1]{0,1:T(1,128)S(1)}, u32[]{:S(2)}) copy-start(s32[512,1]{0,1:T(1,128)S(1)} %compare_select_fusion.1) | copy-start | bytes 6148
  10.8 3.4 %copy-start.1 = (f32[1,32,4096]{2,1,0:T(8,128)S(1)}, f32[1,32,4096]{2,1,0:T(8,128)}, u32[]{:S(2)}) copy-start(f32[1,32,4096]{2,1,0:T(8,128)} %param.6) | copy-start | bytes 1572868
  15.0 62.4 %reduce-scatter.3.cloned.1.call-start = ((), (), s32[]{:S(2)}) async-start(), calls=%async_computation.7 | async-start | bytes 2621440 | tf_op jit(solution)/shard_map/reduce_scatter | solution.py:49
  46.0 0.9 copy-start.2
  46.8 33.3 %copy-start.4 = (s32[1024]{0:T(1024)}, s32[1024]{0:T(1024)S(1)}, u32[]{:S(2)}) copy-start(s32[1024]{0:T(1024)S(1)} %pad_clamp_fusion.1) | copy-start | bytes 12292
  46.9 63.1 %copy-start.6 = (s32[4]{0:T(128)}, s32[4]{0:T(128)S(1)}, u32[]{:S(2)}) copy-start(s32[4]{0:T(128)S(1)} %fusion.65) | copy-start | bytes 52
  81.6 14.3 %all-to-all-start = ((f32[2,32,8,128]{3,1,0,2:T(8,128)}), f32[2,32,8,128]{3,1,0,2:T(8,128)S(1)}, u32[]{:S(2)}, u32[]{:S(2)}) async-start(f32[2,32,8,128]{3,1,0,2:T(8,128)} %copy.83), calls=%async_computation.1 | async-start | bytes 524288 | tf_op jit(solution)/shard_map/all_to_all | solution.py:69
  87.9 13.2 %copy-start.3 = (s32[1024]{0:T(1024)}, s32[1024]{0:T(1024)S(1)}, u32[]{:S(2)}) copy-start(s32[1024]{0:T(1024)S(1)} %broadcast_clamp_fusion) | copy-start | bytes 12292
  106.4 10.9 %all-to-all-start.1 = ((f32[8,32,1,128]{3,1,2,0:T(8,128)}), f32[8,32,1,128]{3,1,2,0:T(8,128)S(1)}, u32[]{:S(2)}, u32[]{:S(2)}) async-start(f32[8,32,1,128]{3,1,2,0:T(8,128)} %constant_dynamic-update-slice_fusion), calls=%async_computation.2 | async-start | bytes 262144 | tf_op jit(solution)/shard_map/all_to_all | solution.py:77
  110.0 28.2 %all-gather.5.cloned.1.call-start = ((), (), s32[]{:S(2)}) async-start(), calls=%async_computation.8 | async-start | bytes 1310720 | tf_op jit(solution)/shard_map/all_gather | solution.py:43
  110.1 12.5 %copy-start.9 = (s32[1024]{0:T(1024)}, s32[1024]{0:T(1024)S(1)}, u32[]{:S(2)}) copy-start(s32[1024]{0:T(1024)S(1)} %pad_clamp_fusion) | copy-start | bytes 12292
  124.5 56.5 %reduce-scatter.5.cloned.1.call-start = ((), (), s32[]{:S(2)}) async-start(), calls=%async_computation.9 | async-start | bytes 2621440 | tf_op jit(solution)/shard_map/reduce_scatter | solution.py:49
  149.7 33.0 %copy-start.5 = (s32[1024]{0:T(1024)S(1)}, s32[1024]{0:T(1024)}, u32[]{:S(2)}) copy-start(s32[1024]{0:T(1024)} %copy-done.4) | copy-start | bytes 12292
  182.1 1.8 copy-start.7
  204.1 9.1 %copy-start = (f32[32,4096]{1,0:T(8,128)S(1)}, f32[32,4096]{1,0:T(8,128)}, u32[]{:S(2)}) copy-start(f32[32,4096]{1,0:T(8,128)} %reduce-scatter.5.cloned.1.call-done) | copy-start | bytes 1572868
  209.7 10.9 %all-to-all-start.3 = ((f32[8,32,1,128]{3,1,2,0:T(8,128)}), f32[8,32,1,128]{3,1,2,0:T(8,128)S(1)}, u32[]{:S(2)}, u32[]{:S(2)}) async-start(f32[8,32,1,128]{3,1,2,0:T(8,128)} %constant_dynamic-update-slice_fusion.8), calls=%async_computation.5 | async-start | bytes 262144 | tf_op jit(solution)/shard_map/all_to_all | solution.py:77
Sparse Core Ops, SparseCore 0:
  15.1 19.4 all-gather.2
  46.1 31.1 reduce-scatter.2
  124.7 13.5 all-gather.4
  149.8 31.1 reduce-scatter.4
